TPU v7x, 256 devices: a whole 4x4x8 slice. The times are simulated.
256 devices in a mesh: req: 32 (over z, y), mdl: 8 (over x, core).
Axes of the slice: x: 4, y: 4, z: 8, core: 2. Of those that a mesh axis runs over, the one named last changes fastest.
Arguments:
- tokens: bfloat16 [8192, 2048], P('req', 'mdl'), may hold values from -6 to 6
- prefix_cache: bfloat16 [16384, 2, 2048], P('req', None, 'mdl'), may hold values from -68 to 68
- qkv_weight: bfloat16 [2048, 3, 2048], P(None, None, 'mdl'), may hold values from -0.125 to 0.125
- out_weight: bfloat16 [2048, 2048], P('mdl'), may hold values from -0.75 to 0.75
- gate_up_weight: bfloat16 [2048, 2, 4096], P(None, None, 'mdl'), may hold values from -0.125 to 0.125
- down_weight: bfloat16 [4096, 2048], P('mdl'), may hold values from -0.09375 to 0.09375
- lengths: int32 [128], replicated, may hold values from 0 to 256, as said below
- placement: int32 [128], replicated, may hold values from 0 to 31, as said below
- request_group: int32 [128], replicated, may hold values from 0 to 3
- block_owner: int32 [32], replicated, may hold values from 0 to 31, each once
- start_position: int32 [128], replicated, may hold values from 4096 to 4351
Outputs:
- out: bfloat16 [8192, 2048], P('req', 'mdl')
Inputs may be any that keep to these rules, and one draw needn't show every extreme that they name: `placement`: each index of req holds exactly 4 requests. The lengths of the requests on one index of req sum to at most 256, and to exactly 256 on some index; all lengths together sum to exactly 128 times the number of indices of req.
All inputs are finite; a program needn't handle non-finite values.
Results may differ from a plain program's by a relative error of at most 0.017.
Values may be sent and summed in bfloat16 or wider, within the bound.
A program may use at most 128 MiB of HBM per device.

v0:
```python
import math

import jax
import jax.numpy as jnp
from jax import lax
from jax.sharding import PartitionSpec as P

HD = 128
G = 4


NEG = -1e30
EPS = 1e-05


def slot_table(lengths, placement, request_group, start_position, device, capacity):
    request_count = lengths.shape[0]
    request_ids = jnp.arange(request_count, dtype=jnp.int32)
    same_device = placement[:, None] == placement[None, :]
    earlier = request_ids[None, :] < request_ids[:, None]
    before = jnp.sum(jnp.where(same_device & earlier, lengths[None, :], 0), axis=1)
    ending = before + lengths
    slot_ids = jnp.arange(capacity, dtype=jnp.int32)
    belongs = (
        (placement[None, :] == device)
        & (slot_ids[:, None] >= before[None, :])
        & (slot_ids[:, None] < ending[None, :])
    )
    occupied = jnp.any(belongs, axis=1)
    request = jnp.sum(jnp.where(belongs, request_ids[None, :], 0), axis=1)
    slot_group = jnp.where(
        occupied, jnp.sum(jnp.where(belongs, request_group[None, :], 0), axis=1), -1
    )
    first_slot = jnp.sum(jnp.where(belongs, before[None, :], 0), axis=1)
    offset = slot_ids - first_slot
    position = jnp.sum(jnp.where(belongs, start_position[None, :], 0), axis=1) + offset
    return (occupied, request, slot_group, offset, position)


def block_groups(block_owner, group_count):
    block_count = block_owner.shape[0]
    per_group = block_count // group_count
    entry_ids = jnp.arange(block_count, dtype=jnp.int32)
    hits = block_owner[None, :] == entry_ids[:, None]
    entry = jnp.sum(jnp.where(hits, entry_ids[None, :], 0), axis=1)
    return entry // per_group


def lookup(values, wanted):
    hits = jnp.arange(values.shape[0], dtype=jnp.int32) == wanted
    return jnp.sum(jnp.where(hits, values, 0))


def rotate(vectors, position):
    half_width = vectors.shape[-1] // 2
    pair_ids = jnp.arange(half_width, dtype=jnp.float32)
    frequency = jnp.exp(pair_ids * (-2.0 * math.log(10000.0) / vectors.shape[-1]))
    angles = position.astype(jnp.float32)[:, None] * frequency[None, :]
    cosine = jnp.cos(angles)[:, None, :]
    sine_part = jnp.sin(angles)[:, None, :]
    lower = vectors[..., :half_width]
    upper = vectors[..., half_width:]
    return jnp.concatenate(
        [lower * cosine - upper * sine_part, upper * cosine + lower * sine_part], axis=-1
    )


def layer_norm(values):
    row_mean = jnp.mean(values, axis=-1, keepdims=True)
    centered = values - row_mean
    row_var = jnp.mean(centered * centered, axis=-1, keepdims=True)
    return centered * lax.rsqrt(row_var + EPS)


def block_partial(queries, key_rows, value_rows, allowed):
    score_scale = queries.shape[-1] ** (-0.5)
    scores = (
        jnp.einsum("shd,khd->hsk", queries, key_rows, preferred_element_type=jnp.float32)
        * score_scale
    )
    scores = jnp.where(allowed[None], scores, NEG)
    row_max = jnp.max(scores, axis=-1)
    weights = jnp.where(allowed[None], jnp.exp(scores - row_max[..., None]), 0.0)
    weight_sum = jnp.sum(weights, axis=-1)
    present = jnp.any(allowed, axis=-1)[None, :]
    safe_sum = jnp.where(present, weight_sum, 1.0)
    mixture = jnp.einsum(
        "hsk,khd->shd", weights.astype(jnp.bfloat16), value_rows, preferred_element_type=jnp.float32
    )
    normalized = (mixture / jnp.transpose(safe_sum)[:, :, None]).astype(jnp.bfloat16)
    log_sum = jnp.where(present, row_max + jnp.log(safe_sum), NEG)
    return (normalized, jnp.transpose(log_sum))


def combine(merged, partial_out, partial_lse):
    weighted, running_max, weight_sum = merged
    new_max = jnp.maximum(running_max, partial_lse)
    old_scale = jnp.exp(running_max - new_max)
    new_scale = jnp.exp(partial_lse - new_max)
    weighted = (
        weighted * old_scale[..., None] + partial_out.astype(jnp.float32) * new_scale[..., None]
    )
    return (weighted, new_max, weight_sum * old_scale + new_scale)


def feed_forward(residual_rows, gate_up_weight, down_weight):
    full_rows = lax.all_gather(residual_rows, "mdl", axis=1, tiled=True)
    normed = layer_norm(full_rows.astype(jnp.float32)).astype(jnp.bfloat16)
    gate_up = jnp.einsum("sd,dtf->stf", normed, gate_up_weight, preferred_element_type=jnp.float32)
    hidden = (jax.nn.silu(gate_up[:, 0]) * gate_up[:, 1]).astype(jnp.bfloat16)
    partial_sums = jnp.dot(hidden, down_weight, preferred_element_type=jnp.float32)
    return lax.psum_scatter(
        partial_sums.astype(jnp.bfloat16), "mdl", scatter_dimension=1, tiled=True
    ).astype(jnp.float32)


def local(
    tokens,
    prefix_cache,
    qkv_weight,
    out_weight,
    gate_up_weight,
    down_weight,
    lengths,
    placement,
    request_group,
    block_owner,
    start_position,
):
    capacity = tokens.shape[0]
    head_width = out_weight.shape[0]
    head_count = head_width // HD
    block_rows = prefix_cache.shape[0]
    device = lax.axis_index("req")
    occupied, request, slot_group, offset, position = slot_table(
        lengths, placement, request_group, start_position, device, capacity
    )
    gathered = lax.all_gather(tokens, "mdl", axis=1, tiled=True)
    normed = layer_norm(gathered.astype(jnp.float32)).astype(jnp.bfloat16)
    projected = jnp.einsum("sd,dtc->stc", normed, qkv_weight, preferred_element_type=jnp.float32)
    queries = rotate(projected[:, 0].reshape(capacity, head_count, HD), position).astype(
        jnp.bfloat16
    )
    key_rows = rotate(projected[:, 1].reshape(capacity, head_count, HD), position).astype(
        jnp.bfloat16
    )
    value_rows = projected[:, 2].reshape(capacity, head_count, HD).astype(jnp.bfloat16)
    group_table = block_groups(block_owner, G)
    start_state = (
        jnp.zeros((capacity, head_count, HD), jnp.float32),
        jnp.full((capacity, head_count), NEG, jnp.float32),
        jnp.zeros((capacity, head_count), jnp.float32),
    )
    merged = start_state
    arrived = lax.all_gather(prefix_cache, "req", axis=0, tiled=True)
    block_count = arrived.shape[0] // block_rows
    blocks = arrived.reshape(block_count, block_rows, 2, head_count, HD)

    def over_blocks(running, element):
        block, block_index = element
        block_group = lookup(group_table, block_index)
        allowed = jnp.broadcast_to((slot_group == block_group)[:, None], (capacity, block_rows))
        partial_out, partial_lse = block_partial(queries, block[:, 0], block[:, 1], allowed)
        return (combine(running, partial_out, partial_lse), None)

    merged, unused = lax.scan(
        over_blocks, merged, (blocks, jnp.arange(block_count, dtype=jnp.int32))
    )
    causal = (
        occupied[:, None]
        & occupied[None, :]
        & (request[:, None] == request[None, :])
        & (offset[None, :] <= offset[:, None])
    )
    partial_out, partial_lse = block_partial(queries, key_rows, value_rows, causal)
    weighted, running_max, weight_sum = combine(merged, partial_out, partial_lse)
    attention = (
        (weighted / weight_sum[..., None]).reshape(capacity, head_width).astype(jnp.bfloat16)
    )
    head_terms = jnp.dot(attention, out_weight, preferred_element_type=jnp.float32)
    residual = (
        tokens.astype(jnp.float32)
        + lax.psum_scatter(
            head_terms.astype(jnp.bfloat16), "mdl", scatter_dimension=1, tiled=True
        ).astype(jnp.float32)
    ).astype(jnp.bfloat16)
    finished = residual.astype(jnp.float32) + feed_forward(residual, gate_up_weight, down_weight)
    return jnp.where(occupied[:, None], finished, 0.0).astype(jnp.bfloat16)


def solution(mesh):
    in_specs = (
        P("req", "mdl"),
        P("req", None, "mdl"),
        P(None, None, "mdl"),
        P("mdl", None),
        P(None, None, "mdl"),
        P("mdl", None),
        P(),
        P(),
        P(),
        P(),
        P(),
    )
    out_specs = P("req", "mdl")
    return jax.shard_map(local, mesh=mesh, in_specs=in_specs, out_specs=out_specs, check_vma=False)
```

profile of v0, /device:TPU:1, one launch (start us, length us, event | category | flops | bytes accessed | tf_op | source)
XLA Modules:
  0.0 524.7 jit_solution(17898964725796724855)
XLA Ops:
  15.4 23.9 %all-gather.6.cloned.1.call-done = bf16[256,2048]{1,0:T(8,128)(2,1)} async-done(((bf16[256,256]{1,0:T(8,128)(2,1)}), bf16[256,2048]{1,0:T(8,128)(2,1)}) %all-gather.6.cloned.1.call-update) | async-done | bytes 1048592 | tf_op jit(solution)/shard_map/all_gather | solution.py:138
  39.3 1.5 convert_reduce_fusion.1
  40.8 1.6 fusion.26
  42.5 1.5 fusion.37
  47.2 1.7 fusion.75
  48.9 1.7 copy.66
  50.6 1.7 copy.67
  52.4 1.7 copy.65
  58.5 124.2 %all-gather.4.cloned.1.call-done = bf16[16384,2,256]{2,1,0:T(2,128)(2,1)} async-done(((bf16[512,2,256]{2,1,0:T(2,128)(2,1)}), bf16[16384,2,256]{2,1,0:T(2,128)(2,1)}) %all-gather.4.cloned.1.call-update) | async-done | bytes 16777232 | tf_op jit(solution)/shard_map/all_gather | solution.py:155
  182.8 41.4 %reshape.208 = bf16[32,512,2,2,128]{4,3,2,1,0:T(2,128)(2,1)} reshape(bf16[16384,2,256]{2,1,0:T(2,128)(2,1)} %all-gather.4.cloned.1.call-done) | data formatting | bytes 33554432 | tf_op jit(solution)/shard_map/reshape | solution.py:157
  224.2 188.9 %while.15 = (s32[]{:T(128)}, f32[256,2,128]{0,2,1:T(8,128)}, f32[256,2]{0,1:T(2,128)S(1)}, f32[256,2]{0,1:T(2,128)S(1)}, s32[32]{0:T(128)S(1)}, /*index=5*/s32[3...) while((s32[]{:T(128)}, f32[256,2,128]{0,2,1:T(8,128)}, ...), condition=%wide.region_13.14_spmd.clone, body=%wide.region_8.0_spmd.clone.sunk | while | flops 137171552 | bytes 8558420 | solution.py:166
  227.0 1.5 constant_dynamic-slice_fusion.2
  238.8 1.5 constant_dynamic-slice_fusion.2
  244.7 1.5 constant_dynamic-slice_fusion.2
  250.6 1.5 constant_dynamic-slice_fusion.2
  256.5 1.5 constant_dynamic-slice_fusion.2
  262.4 1.5 constant_dynamic-slice_fusion.2
  268.3 1.5 constant_dynamic-slice_fusion.2
  274.2 1.5 constant_dynamic-slice_fusion.2
  280.1 1.5 constant_dynamic-slice_fusion.2
  286.0 1.5 constant_dynamic-slice_fusion.2
  291.9 1.5 constant_dynamic-slice_fusion.2
  297.8 1.5 constant_dynamic-slice_fusion.2
  303.7 1.5 constant_dynamic-slice_fusion.2
  309.6 1.5 constant_dynamic-slice_fusion.2
  315.5 1.5 constant_dynamic-slice_fusion.2
  321.4 1.5 constant_dynamic-slice_fusion.2
  327.3 1.5 constant_dynamic-slice_fusion.2
  339.1 1.5 constant_dynamic-slice_fusion.2
  345.0 1.5 constant_dynamic-slice_fusion.2
  350.9 1.5 constant_dynamic-slice_fusion.2
  356.8 1.5 constant_dynamic-slice_fusion.2
  362.7 1.5 constant_dynamic-slice_fusion.2
  368.6 1.5 constant_dynamic-slice_fusion.2
  374.5 1.5 constant_dynamic-slice_fusion.2
  380.4 1.5 constant_dynamic-slice_fusion.2
  386.3 1.5 constant_dynamic-slice_fusion.2
  392.2 1.5 constant_dynamic-slice_fusion.2
  398.1 1.5 constant_dynamic-slice_fusion.2
  416.2 29.5 %reduce-scatter.3.cloned.1.call-done = bf16[256,256]{1,0:T(8,128)(2,1)} async-done(((bf16[256,2048]{1,0:T(8,128)(2,1)}), bf16[256,256]{1,0:T(8,128)(2,1)}) %reduce-scatter.3.cloned.1.call-update) | async-done | bytes 131088 | tf_op jit(solution)/shard_map/reduce_scatter | solution.py:183
  445.7 1.6 add_convert_fusion
  447.4 27.7 %all-gather.8.cloned.1.call-done = bf16[256,2048]{1,0:T(8,128)(2,1)} async-done(((bf16[256,256]{1,0:T(8,128)(2,1)}), bf16[256,2048]{1,0:T(8,128)(2,1)}) %all-gather.8.cloned.1.call-update) | async-done | bytes 1048592 | tf_op jit(solution)/shard_map/all_gather | solution.py:107
  475.0 1.5 convert_reduce_fusion
  476.6 1.6 fusion.24
  478.3 3.7 fusion.18
  481.9 1.8 convolution_convert_fusion
  483.7 32.8 %reduce-scatter.5.cloned.1.call-done = bf16[256,256]{1,0:T(8,128)(2,1)} async-done(((bf16[256,2048]{1,0:T(8,128)(2,1)}), bf16[256,256]{1,0:T(8,128)(2,1)}) %reduce-scatter.5.cloned.1.call-update) | async-done | bytes 131088 | tf_op jit(solution)/shard_map/reduce_scatter | solution.py:112
  516.5 1.7 select_convert_fusion
  (521 shorter events, 165.9 us)
Async XLA Ops:
  6.5 36.0 %copy-start = (bf16[2048,3,256]{2,0,1:T(8,128)(2,1)S(1)}, bf16[2048,3,256]{2,0,1:T(8,128)(2,1)}, u32[]{:S(2)}) copy-start(bf16[2048,3,256]{2,0,1:T(8,128)(2,1)} %param.15) | copy-start | bytes 9437188
  6.5 32.8 %all-gather.6.cloned.1.call-start = ((), (), s32[]{:S(2)}) async-start(), calls=%async_computation.3 | async-start | bytes 1179648 | tf_op jit(solution)/shard_map/all_gather | solution.py:138
  7.3 175.5 %all-gather.4.cloned.1.call-start = ((), (), s32[]{:S(2)}) async-start(), calls=%async_computation.2 | async-start | bytes 17301504 | tf_op jit(solution)/shard_map/all_gather | solution.py:155
  8.0 437.7 %reduce-scatter.3.cloned.1.call-start = ((), (), s32[]{:S(2)}) async-start(), calls=%async_computation.4 | async-start | bytes 1179648 | tf_op jit(solution)/shard_map/reduce_scatter | solution.py:183
  39.3 3.2 copy-start.1
  54.1 4.4 copy-start.9
  58.5 165.6 %copy-start.14 = (s32[32]{0:T(128)S(1)}, s32[32]{0:T(128)}, u32[]{:S(2)}) copy-start(s32[32]{0:T(128)} %and_select_fusion) | copy-start | bytes 388
  224.2 188.9 %copy-start.10 = (pred[256]{0:T(512)(128)(4,1)S(1)}, pred[256]{0:T(512)(128)(4,1)}, u32[]{:S(2)}) copy-start(pred[256]{0:T(512)(128)(4,1)} %get-tuple-element.157) | copy-start | bytes 772
  224.2 189.0 %copy-start.6 = (pred[256,256]{0,1:T(8,128)(4,1)S(1)}, pred[256,256]{0,1:T(8,128)(4,1)}, u32[]{:S(2)}) copy-start(pred[256,256]{0,1:T(8,128)(4,1)} %copy.53) | copy-start | bytes 196612
  224.2 189.0 %copy-start.8 = (bf16[256,1,256]{0,2,1:T(8,128)(2,1)S(1)}, bf16[256,1,256]{0,2,1:T(8,128)(2,1)}, u32[]{:S(2)}) copy-start(bf16[256,1,256]{0,2,1:T(8,128)(2,1)} %slice.71) | copy-start | bytes 393220
  227.0 2.1 copy-start.12
  232.9 2.1 copy-start.12
  238.8 2.1 copy-start.12
  244.7 2.1 copy-start.12
  250.6 2.1 copy-start.12
  256.5 2.1 copy-start.12
  262.4 2.1 copy-start.12
  268.3 2.1 copy-start.12
  274.2 2.1 copy-start.12
  280.1 2.1 copy-start.12
  286.0 2.1 copy-start.12
  291.9 2.1 copy-start.12
  297.8 2.1 copy-start.12
  303.7 2.1 copy-start.12
  309.6 2.1 copy-start.12
  315.5 2.1 copy-start.12
  321.4 2.1 copy-start.12
  327.3 2.1 copy-start.12
  333.2 2.1 copy-start.12
  339.1 2.1 copy-start.12
  345.0 2.1 copy-start.12
  350.9 2.1 copy-start.12
  356.8 2.1 copy-start.12
  362.7 2.1 copy-start.12
  368.6 2.1 copy-start.12
  374.5 2.1 copy-start.12
  380.4 2.1 copy-start.12
  386.3 2.1 copy-start.12
  392.2 2.1 copy-start.12
  398.1 2.1 copy-start.12
  404.0 2.1 copy-start.12
  409.9 2.1 copy-start.12
  414.6 31.1 %copy-start.7 = (bf16[256,256]{1,0:T(8,128)(2,1)S(1)}, bf16[256,256]{1,0:T(8,128)(2,1)}, u32[]{:S(2)}) copy-start(bf16[256,256]{1,0:T(8,128)(2,1)} %param.13) | copy-start | bytes 393220
  416.1 58.9 %all-gather.8.cloned.1.call-start = ((), (), s32[]{:S(2)}) async-start(), calls=%async_computation.5 | async-start | bytes 1179648 | tf_op jit(solution)/shard_map/all_gather | solution.py:107
  447.3 69.2 %reduce-scatter.5.cloned.1.call-start = ((), (), s32[]{:S(2)}) async-start(), calls=%async_computation.6 | async-start | bytes 1179648 | tf_op jit(solution)/shard_map/reduce_scatter | solution.py:112
  475.0 3.2 copy-start.2
  478.2 3.7 copy-start.11
  481.9 34.6 %copy-start.4 = (bf16[256,256]{1,0:T(8,128)(2,1)S(1)}, bf16[256,256]{1,0:T(8,128)(2,1)}, u32[]{:S(2)}) copy-start(bf16[256,256]{1,0:T(8,128)(2,1)} %add_convert_fusion) | copy-start | bytes 393220
  (34 other events, 24.5 us)
Sparse Core Ops, SparseCore 0:
  9.2 30.0 all-gather.5
  41.9 140.8 all-gather.3
  416.2 29.4 reduce-scatter.2
  447.4 27.5 all-gather.7
  483.8 32.6 reduce-scatter.4
where the time goes:
time: 529 us; the launch traced here: 525 us
  waiting for transfers between devices  240 us (45%)
  local copies, waits for them, and re-layouts  145 us (27%)
  other arithmetic  91.8 us (17%)
  matrix products  32.9 us (6%)
  between operations  13.4 us (3%)
    all_gather x1, waiting for transfers between devices, local(): arrived = lax.all_gather(prefix_cache, 'req', axis=0, tiled=True)  124 us
    dynamic_slice x96, local copies, waits for them, and re-layouts, local(): lax.scan(over_blocks, merged, (blocks, jnp.arange(block_count, dtype=jnp....  69.9 us
    reduce_sum x32, other arithmetic, lookup(): return jnp.sum(jnp.where(hits, values, 0))  42 us
    reshape x1, local copies, waits for them, and re-layouts, local(): blocks = arrived.reshape(block_count, block_rows, 2, head_count, HD)  41.4 us
    reduce_scatter x1, waiting for transfers between devices, feed_forward(): lax.psum_scatter(partial_sums.astype(jnp.bfloat16), 'mdl', scatter_dimens...  32.8 us
    reduce_scatter x1, waiting for transfers between devices, local(): lax.psum_scatter(head_terms.astype(jnp.bfloat16), 'mdl', scatter_dimensio...  29.5 us
    all_gather x1, waiting for transfers between devices, feed_forward(): full_rows = lax.all_gather(residual_rows, 'mdl', axis=1, tiled=True)  27.7 us
    all_gather x1, waiting for transfers between devices, local(): gathered = lax.all_gather(tokens, 'mdl', axis=1, tiled=True)  23.9 us
  transfers between devices with their start and end apart: 5, of which 5 were waited for; matrix products, arithmetic and copies ran while one was open for 5% of the time, Pallas kernels for 0%

commit v1 on v0

v1 whole, which is shorter than its diff:
```python
import functools
import math

import jax
import jax.numpy as jnp
from jax import lax
from jax.experimental import pallas as pl
from jax.experimental.pallas import tpu as pltpu
from jax.sharding import PartitionSpec as P

HD = 128
NEG = -1e30
EPS = 1e-05
NX, NY, NZ = 4, 4, 8
MESH = pl.DeviceIdType.MESH
F32 = jnp.float32
BF16 = jnp.bfloat16


def dot(a, b):
    return jnp.dot(a, b, preferred_element_type=F32)


def layer_kernel(
    tok, kc, vc, lens, place, group, start, owner, wqkv, wo, wg, wu, wd,
    out,
    tokg, resg, normed, wqkv_v, wo_v, wg_v, wu_v, wd_v,
    kbuf, vtbuf, qbuf, kloc, vtloc, s_scr, part_acc, part_stat, suf_acc, suf_stat,
    rin_acc, rin_stat, rout_acc, rout_stat, grp_scr, bg_scr,
    pair_out, pair_in, stage, ain, lin, rin, mine, res_own,
    wsem, kv_s, kv_r, q_s, q_r, ra_s, ra_r, rs_s, rs_r,
    ag_s, ag_r, sc_s, sc_r,
):
    cap = tok.shape[0]
    width = tok.shape[1]
    req = lax.axis_index("req")
    mdl = lax.axis_index("mdl")
    z = req // NY
    y = req % NY
    x = mdl // 2
    c = mdl % 2
    xr, xl, xa = (x + 1) % NX, (x + NX - 1) % NX, (x + 2) % NX
    yr, yl, ya = (y + 1) % NY, (y + NY - 1) % NY, (y + 2) % NY
    zr, zl = (z + 1) % NZ, (z + NZ - 1) % NZ
    sib = (req, x * 2 + (1 - c))
    x_right = (req, xr * 2 + c)
    x_left = (req, xl * 2 + c)
    y_right = (z * NY + yr, mdl)
    y_left = (z * NY + yl, mdl)
    z_right = (zr * NY + y, mdl)
    z_left = (zl * NY + y, mdl)
    pending = []

    def send(src, dst, s_sem, r_sem, device):
        copy = pltpu.make_async_remote_copy(
            src_ref=src, dst_ref=dst, send_sem=s_sem, recv_sem=r_sem,
            device_id=device, device_id_type=MESH,
        )
        copy.start()
        pending.append(copy)
        return copy

    loads = []
    for i, (src, dst) in enumerate(
        ((wqkv, wqkv_v), (wo, wo_v), (wg, wg_v), (wu, wu_v), (wd, wd_v))
    ):
        load = pltpu.make_async_copy(src, dst, wsem.at[i])
        load.start()
        loads.append(load)

    barrier = pltpu.get_barrier_semaphore()
    for device in (sib, x_right, x_left, y_right, y_left, z_right, z_left):
        pl.semaphore_signal(barrier, inc=1, device_id=device, device_id_type=MESH)
    pl.semaphore_wait(barrier, 7)

    class Gather:
        def __init__(self, buf, n):
            self.buf, self.n = buf, n
            s, r = ag_s.at[n], ag_r.at[n]
            self.s, self.r = s, r
            own = buf.at[mdl]
            self.c_right = send(own, own, s.at[0], r.at[0], x_right)
            self.c_left = send(own, own, s.at[1], r.at[1], x_left)
            self.c_sib = send(own, own, s.at[2], r.at[2], sib)

        def finish(self):
            buf, s, r = self.buf, self.s, self.r
            half = cap // 2
            from_left, from_right, far = xl * 2 + c, xr * 2 + c, xa * 2 + c
            low, high = pl.ds(0, half), pl.ds(half, half)
            self.c_right.wait_recv()
            f_right = send(buf.at[from_left, low], buf.at[from_left, low], s.at[3], r.at[3], x_right)
            s_left = send(buf.at[from_left], buf.at[from_left], s.at[4], r.at[4], sib)
            self.c_left.wait_recv()
            f_left = send(buf.at[from_right, high], buf.at[from_right, high], s.at[5], r.at[5], x_left)
            s_right = send(buf.at[from_right], buf.at[from_right], s.at[6], r.at[6], sib)
            f_right.wait_recv()
            s_low = send(buf.at[far, low], buf.at[far, low], s.at[7], r.at[7], sib)
            f_left.wait_recv()
            s_high = send(buf.at[far, high], buf.at[far, high], s.at[8], r.at[8], sib)
            for copy in (self.c_sib, s_left, s_right, s_low, s_high):
                copy.wait_recv()

    def reduce_scatter(n, chunk):
        half = cap // 2
        low, high = pl.ds(0, half), pl.ds(half, half)
        s, r = sc_s.at[n], sc_r.at[n]
        order = (xa, xr, xl, x)
        pairs = []
        for i, xd in enumerate(order):
            pair_out[n, i] = chunk(xd * 2 + (1 - c)).astype(BF16)
            pairs.append(send(pair_out.at[n, i], pair_in.at[n, i], s.at[i], r.at[i], sib))

        def combined(i):
            own = chunk(order[i] * 2 + c)
            pairs[i].wait_recv()
            return own + pair_in[n, i].astype(F32)

        stage[n, 0] = combined(0).astype(BF16)
        a_low = send(stage.at[n, 0, low], ain.at[n, low], s.at[4], r.at[4], x_right)
        a_high = send(stage.at[n, 0, high], ain.at[n, high], s.at[5], r.at[5], x_left)
        to_right = combined(1)
        mine[0] = to_right[:half]
        stage[n, 1, high] = to_right[half:].astype(BF16)
        b_high = send(stage.at[n, 1, high], lin.at[n, high], s.at[6], r.at[6], x_right)
        to_left = combined(2)
        mine[1] = to_left[half:]
        stage[n, 2, low] = to_left[:half].astype(BF16)
        b_low = send(stage.at[n, 2, low], rin.at[n, low], s.at[7], r.at[7], x_left)
        own = combined(3)
        mine[2] = own[:half]
        mine[3] = own[half:]
        a_low.wait_recv()
        stage[n, 1, low] = (mine[0] + ain[n, low].astype(F32)).astype(BF16)
        d_low = send(stage.at[n, 1, low], lin.at[n, low], s.at[8], r.at[8], x_right)
        a_high.wait_recv()
        stage[n, 2, high] = (mine[1] + ain[n, high].astype(F32)).astype(BF16)
        d_high = send(stage.at[n, 2, high], rin.at[n, high], s.at[9], r.at[9], x_left)
        for copy in (b_high, b_low, d_low, d_high):
            copy.wait_recv()
        return (
            mine[2] + lin[n, low].astype(F32) + rin[n, low].astype(F32),
            mine[3] + lin[n, high].astype(F32) + rin[n, high].astype(F32),
        )

    def normalize(buf):
        total = jnp.zeros((cap, width), F32)
        for i in range(8):
            total += buf[i].astype(F32)
        mean = jnp.sum(total, axis=1, keepdims=True) * (1.0 / (8 * width))
        square = jnp.zeros((cap, width), F32)
        for i in range(8):
            centered = buf[i].astype(F32) - mean
            square += centered * centered
        var = jnp.sum(square, axis=1, keepdims=True) * (1.0 / (8 * width))
        scale = lax.rsqrt(var + EPS)
        for i in range(8):
            normed[:, i * width : (i + 1) * width] = ((buf[i].astype(F32) - mean) * scale).astype(BF16)

    tokg[mdl] = tok[...]
    gather_tokens = Gather(tokg, 0)
    for h in range(2):
        cols = slice(h * HD, (h + 1) * HD)
        kbuf[0, h] = kc[:, cols]
    k_right = send(kbuf.at[0], kbuf.at[1], kv_s.at[0], kv_r.at[0], y_right)
    k_left = send(kbuf.at[0], kbuf.at[2], kv_s.at[1], kv_r.at[1], y_left)
    for h in range(2):
        cols = slice(h * HD, (h + 1) * HD)
        vtbuf[0, h] = jnp.transpose(vc[:, cols].astype(F32)).astype(BF16)
    v_left = send(vtbuf.at[0], vtbuf.at[2], kv_s.at[2], kv_r.at[2], y_left)
    v_right = send(vtbuf.at[0], vtbuf.at[1], kv_s.at[3], kv_r.at[3], y_right)

    count = lens.shape[1]
    ring = lax.broadcasted_iota(jnp.int32, (8, count), 0)
    ring_device = ((z - ring + NZ) % NZ) * NY + y
    placed = place[...] == ring_device
    held = jnp.where(placed, lens[...], 0).astype(F32)
    upper = (
        lax.broadcasted_iota(jnp.int32, (count, count), 0)
        < lax.broadcasted_iota(jnp.int32, (count, count), 1)
    )
    before = dot(held.astype(BF16), jnp.where(upper, 1.0, 0.0).astype(BF16))
    columns = jnp.transpose(
        jnp.concatenate([before, held, jnp.zeros((count - 16, count), F32)], axis=0)
    )
    row = lax.broadcasted_iota(jnp.int32, (8, count), 0)
    request = lax.broadcasted_iota(jnp.int32, (8, count), 1).astype(F32)
    start_high = jnp.right_shift(start[...], 8).astype(F32)
    start_low = jnp.bitwise_and(start[...], 255).astype(F32)
    values = jnp.where(row == 0, 1.0, 0.0)
    values = jnp.where(row == 1, group[...].astype(F32), values)
    values = jnp.where(row == 2, request, values)
    values = jnp.where(row == 3, start_high, values)
    values = jnp.where(row == 4, start_low, values)
    values = jnp.where(row == 5, jnp.broadcast_to(before[0:1], (8, count)), values)
    values = values.astype(BF16)
    slot = lax.broadcasted_iota(jnp.int32, (count, cap), 1).astype(F32)
    for r in range(NZ):
        first = columns[:, r : r + 1]
        size = columns[:, 8 + r : 9 + r]
        belongs = jnp.where((slot >= first) & (slot < first + size), 1.0, 0.0).astype(BF16)
        table = dot(values, belongs)
        slot_group = jnp.where(table[0:1] > 0.5, table[1:2], -1.0)
        grp_scr[r] = jnp.broadcast_to(slot_group, (8, cap))
        if r == 0:
            own_table = table
    occupied = own_table[0:1]
    slot_request = jnp.where(occupied > 0.5, own_table[2:3], -1.0)
    position = (
        own_table[3:4] * 256.0
        + own_table[4:5]
        + (lax.broadcasted_iota(jnp.int32, (1, cap), 1).astype(F32) - own_table[5:6])
    )
    live = jnp.sum(held[0:1], axis=1, keepdims=True)
    blocks = lax.broadcasted_iota(jnp.int32, (1, owner.shape[1]), 1)
    for b, yb in enumerate((y, yl, yr, ya)):
        mine_block = owner[...] == z * NY + yb
        entry = jnp.where(mine_block, jnp.right_shift(blocks, 3), 0).astype(F32)
        bg_scr[b] = jnp.broadcast_to(jnp.sum(entry, axis=1, keepdims=True), (8, cap))
    pair = lax.broadcasted_iota(jnp.int32, (HD // 2, cap), 0).astype(F32)
    frequency = jnp.exp(pair * (-2.0 * math.log(10000.0) / HD))
    angles = position * frequency
    cosine = jnp.cos(angles)
    sine = jnp.sin(angles)

    gather_tokens.finish()
    normalize(tokg)
    loads[0].wait()

    def rotated(p, h):
        flat = jnp.transpose(dot(normed[...], wqkv_v[p, :, h * HD : (h + 1) * HD]))
        lower, higher = flat[: HD // 2], flat[HD // 2 :]
        return jnp.concatenate(
            [lower * cosine - higher * sine, higher * cosine + lower * sine], axis=0
        )

    factor = math.log2(math.e) * HD ** (-0.5)
    for h in range(2):
        qbuf[0, h] = (rotated(0, h) * factor).astype(BF16)

    q_copies = {}

    def q_step(k):
        for h in range(2):
            if k < 4 or h == 0:
                q_copies[0, k, h] = send(
                    qbuf.at[k - 1, h], qbuf.at[k, h], q_s.at[0, k, h], q_r.at[0, k, h], z_right
                )
            if k < 4 or h == 1:
                q_copies[1, k, h] = send(
                    qbuf.at[(NZ + 1 - k) % NZ, h], qbuf.at[NZ - k, h],
                    q_s.at[1, k, h], q_r.at[1, k, h], z_left,
                )

    def q_wait(k):
        for h in range(2):
            for d in range(2):
                if (d, k, h) in q_copies:
                    q_copies[d, k, h].wait_recv()

    q_step(1)

    for h in range(2):
        kloc[h] = jnp.transpose(rotated(1, h)).astype(BF16)
        vtloc[h] = jnp.transpose(dot(normed[...], wqkv_v[2, :, h * HD : (h + 1) * HD])).astype(BF16)

    k_right.wait_recv()
    fk = send(kbuf.at[1], kbuf.at[3], kv_s.at[4], kv_r.at[4], y_right)
    v_left.wait_recv()
    fv = send(vtbuf.at[2], vtbuf.at[3], kv_s.at[5], kv_r.at[5], y_left)

    def put_stat(ref, top, weight):
        which = lax.broadcasted_iota(jnp.int32, (8, cap), 0)
        ref[...] = jnp.where(which == 0, top, jnp.where(which == 1, weight, 0.0))

    request_column = jnp.transpose(jnp.broadcast_to(slot_request, (HD, cap)))[:, 0:1]
    key_slot = lax.broadcasted_iota(jnp.int32, (cap, cap), 0)
    query_slot = lax.broadcasted_iota(jnp.int32, (cap, cap), 1)
    causal = (request_column == slot_request) & (key_slot <= query_slot) & (slot_request >= 0.0)
    for h in range(2):
        scores = jnp.where(causal, dot(kloc[h], qbuf[0, h]), NEG)
        top = jnp.max(scores, axis=0, keepdims=True)
        weights = jnp.where(causal, jnp.exp2(scores - top), 0.0)
        suf_acc[h] = dot(vtloc[h], weights.astype(BF16))
        put_stat(suf_stat.at[h], top, jnp.sum(weights, axis=0, keepdims=True))

    q_wait(1)
    q_step(2)
    k_left.wait_recv()
    v_right.wait_recv()
    fk.wait_recv()
    fv.wait_recv()

    def attend(r, h):
        query = qbuf[r, h]
        slot_groups = grp_scr[r]
        top = jnp.full((8, cap), NEG, F32)
        for b in range(NY):
            scores = dot(kbuf[b, h], query)
            s_scr[b] = scores
            best = jnp.broadcast_to(jnp.max(scores, axis=0, keepdims=True), (8, cap))
            top = jnp.maximum(top, jnp.where(slot_groups == bg_scr[b], best, NEG))
        total = jnp.zeros((1, cap), F32)
        acc = jnp.zeros((HD, cap), F32)
        for b in range(NY):
            shift = jnp.where(slot_groups == bg_scr[b], top, -NEG)[0:1]
            weights = jnp.exp2(s_scr[b] - shift)
            total += jnp.sum(weights, axis=0, keepdims=True)
            acc += dot(vtbuf[b, h], weights.astype(BF16))
        part_acc[r, h] = acc
        put_stat(part_stat.at[r, h], top[0:1], total)

    def attend_both(k, h):
        def body(i, carry):
            attend(jnp.where(i == 0, k, NZ - k), h)
            return carry

        lax.fori_loop(0, 2, body, 0)

    def attend_heads(r):
        def body(h, carry):
            attend(r, h)
            return carry

        lax.fori_loop(0, 2, body, 0)

    attend_both(1, 0)
    q_wait(2)
    q_step(3)
    attend_both(1, 1)
    attend_both(2, 0)
    q_wait(3)
    q_step(4)
    attend_both(2, 1)
    q_wait(4)
    attend_heads(4)

    def combine(parts):
        top = parts[0][1]
        for part in parts[1:]:
            top = jnp.maximum(top, part[1])
        acc, total = 0.0, 0.0
        for part in parts:
            scale = jnp.exp2(part[1] - top)
            acc = acc + part[0] * scale
            total = total + part[2] * scale
        return acc, top, total

    def own_part(r, h):
        return part_acc[r, h], part_stat[r, h, 0:1], part_stat[r, h, 1:2]

    back = {}

    def arrived(d, k, h):
        for copy in back[d, k, h]:
            copy.wait_recv()
        return rin_acc[d, k, h].astype(F32), rin_stat[d, k, h, 0:1], rin_stat[d, k, h, 1:2]

    def back_step(d, k, h):
        parts = [own_part(NZ - k if d == 0 else k, h)]
        if (d, k + 1, h) in back:
            parts.append(arrived(d, k + 1, h))
        acc, top, total = combine(parts)
        rout_acc[d, k, h] = acc.astype(BF16)
        put_stat(rout_stat.at[d, k, h], top, total)
        device = z_right if d == 0 else z_left
        back[d, k, h] = (
            send(rout_acc.at[d, k, h], rin_acc.at[d, k, h], ra_s.at[d, k, h], ra_r.at[d, k, h], device),
            send(rout_stat.at[d, k, h], rin_stat.at[d, k, h], rs_s.at[d, k, h], rs_r.at[d, k, h], device),
        )

    back_step(0, 4, 0)
    back_step(1, 4, 1)
    attend_both(3, 1)
    back_step(0, 3, 1)
    attend_both(3, 0)
    back_step(1, 3, 0)
    back_step(0, 3, 0)
    back_step(1, 3, 1)
    attend_heads(0)
    for k in (2, 1):
        back_step(0, k, 1)
        back_step(1, k, 0)
        back_step(0, k, 0)
        back_step(1, k, 1)
    rows = []
    for h in range(2):
        suffix = (suf_acc[h], suf_stat[h, 0:1], suf_stat[h, 1:2])
        acc, top, total = combine([own_part(0, h), suffix, arrived(0, 1, h), arrived(1, 1, h)])
        some = total > 0.0
        rows.append(jnp.where(some, acc / jnp.where(some, total, 1.0), 0.0))
    attention = jnp.transpose(jnp.concatenate(rows, axis=0)).astype(BF16)

    loads[1].wait()
    normed[:, 0:width] = attention

    def head_chunk(m):
        return dot(normed[:, 0:width], wo_v[:, pl.ds(pl.multiple_of(m * width, width), width)])

    half = cap // 2
    low, high = reduce_scatter(0, head_chunk)
    resg[mdl, 0:half] = (tok[0:half].astype(F32) + low).astype(BF16)
    resg[mdl, half:cap] = (tok[half:cap].astype(F32) + high).astype(BF16)
    res_own[...] = resg[mdl]

    gather_residual = Gather(resg, 1)
    for load in loads[2:]:
        load.wait()
    gather_residual.finish()
    normalize(resg)
    gate = dot(normed[...], wg_v[...])
    up = dot(normed[...], wu_v[...])
    hidden = (gate / (1.0 + jnp.exp(-gate)) * up).astype(BF16)
    normed[:, 0 : 2 * width] = hidden

    def down_chunk(m):
        return dot(
            normed[:, 0 : 2 * width], wd_v[:, pl.ds(pl.multiple_of(m * width, width), width)]
        )

    low, high = reduce_scatter(1, down_chunk)
    index = lax.broadcasted_iota(jnp.int32, (half, width), 0).astype(F32)
    out[0:half] = jnp.where(index < live, res_own[0:half].astype(F32) + low, 0.0).astype(BF16)
    out[half:cap] = jnp.where(
        index + half < live, res_own[half:cap].astype(F32) + high, 0.0
    ).astype(BF16)
    for copy in pending:
        copy.wait_send()


def local(
    tokens, prefix_cache, qkv_weight, out_weight, gate_up_weight, down_weight,
    lengths, placement, request_group, block_owner, start_position,
):
    cap, width = tokens.shape
    block = prefix_cache.shape[0]
    model = qkv_weight.shape[0]
    hidden = down_weight.shape[0]
    vmem = pl.BlockSpec(memory_space=pltpu.VMEM)
    hbm = pl.BlockSpec(memory_space=pl.ANY)
    dma = pltpu.SemaphoreType.DMA
    ring = (2, 5, 2)
    scratch = [
        pltpu.VMEM((8, cap, width), BF16),
        pltpu.VMEM((8, cap, width), BF16),
        pltpu.VMEM((cap, model), BF16),
        pltpu.VMEM((3, model, width), BF16),
        pltpu.VMEM((width, model), BF16),
        pltpu.VMEM((model, hidden), BF16),
        pltpu.VMEM((model, hidden), BF16),
        pltpu.VMEM((hidden, model), BF16),
        pltpu.VMEM((NY, 2, block, HD), BF16),
        pltpu.VMEM((NY, 2, HD, block), BF16),
        pltpu.VMEM((NZ, 2, HD, cap), BF16),
        pltpu.VMEM((2, cap, HD), BF16),
        pltpu.VMEM((2, HD, cap), BF16),
        pltpu.VMEM((NY, block, cap), F32),
        pltpu.VMEM((NZ, 2, HD, cap), F32),
        pltpu.VMEM((NZ, 2, 8, cap), F32),
        pltpu.VMEM((2, HD, cap), F32),
        pltpu.VMEM((2, 8, cap), F32),
        pltpu.VMEM(ring + (HD, cap), BF16),
        pltpu.VMEM(ring + (8, cap), F32),
        pltpu.VMEM(ring + (HD, cap), BF16),
        pltpu.VMEM(ring + (8, cap), F32),
        pltpu.VMEM((NZ, 8, cap), F32),
        pltpu.VMEM((NY, 8, cap), F32),
        pltpu.VMEM((2, 4, cap, width), BF16),
        pltpu.VMEM((2, 4, cap, width), BF16),
        pltpu.VMEM((2, 3, cap, width), BF16),
        pltpu.VMEM((2, cap, width), BF16),
        pltpu.VMEM((2, cap, width), BF16),
        pltpu.VMEM((2, cap, width), BF16),
        pltpu.VMEM((4, cap // 2, width), F32),
        pltpu.VMEM((cap, width), BF16),
        dma((5,)),
        dma((6,)), dma((6,)),
        dma(ring), dma(ring),
        dma(ring), dma(ring), dma(ring), dma(ring),
        dma((2, 9)), dma((2, 9)), dma((2, 10)), dma((2, 10)),
    ]
    return pl.pallas_call(
        layer_kernel,
        out_shape=jax.ShapeDtypeStruct((cap, width), BF16),
        in_specs=[vmem] * 8 + [hbm] * 5,
        out_specs=vmem,
        scratch_shapes=scratch,
        compiler_params=pltpu.CompilerParams(
            collective_id=0, has_side_effects=True, vmem_limit_bytes=58 << 20
        ),
        name="layer",
    )(
        tokens,
        prefix_cache[:, 0],
        prefix_cache[:, 1],
        lengths.reshape(1, -1),
        placement.reshape(1, -1),
        request_group.reshape(1, -1),
        start_position.reshape(1, -1),
        block_owner.reshape(1, -1),
        jnp.transpose(qkv_weight, (1, 0, 2)),
        out_weight,
        gate_up_weight[:, 0],
        gate_up_weight[:, 1],
        down_weight,
    )


def solution(mesh):
    in_specs = (
        P("req", "mdl"),
        P("req", None, "mdl"),
        P(None, None, "mdl"),
        P("mdl", None),
        P(None, None, "mdl"),
        P("mdl", None),
        P(),
        P(),
        P(),
        P(),
        P(),
    )
    return jax.shard_map(
        local, mesh=mesh, in_specs=in_specs, out_specs=P("req", "mdl"), check_vma=False
    )
```

time: 529 us -> 109 us (0.21)
  waiting for transfers between devices: 240 us -> 0 us
  local copies, waits for them, and re-layouts: 145 us -> 15.2 us
  Pallas kernels: 0 us -> 93.5 us
  other arithmetic: 91.8 us -> 0 us
  matrix products: 32.9 us -> 0 us
  between operations: 13.4 us -> 0.03 us
    all_gather x3 -> x0, waiting for transfers between devices: 176 us -> none  [the longest x1 124 us: local(): arrived = lax.all_gather(prefix_cache, 'req', axis=0, tiled=True)]
    pallas_call x0 -> x1, Pallas kernels: none -> 93.5 us  [local(): pl.pallas_call(layer_kernel, out_shape=jax.ShapeDtypeStruct((cap, width),...]
    dynamic_slice x96 -> x0, local copies, waits for them, and re-layouts: 69.9 us -> none  [local(): lax.scan(over_blocks, merged, (blocks, jnp.arange(block_count, dtype=jnp....]
    reduce_scatter x2 -> x0, waiting for transfers between devices: 62.3 us -> none  [the longest x1 32.8 us: feed_forward(): lax.psum_scatter(partial_sums.astype(jnp.bfloat16), 'mdl', scatter_dimens...]
    reduce_sum x72 -> x0, other arithmetic: 58 us -> none  [the longest x32 42 us: lookup(): return jnp.sum(jnp.where(hits, values, 0))]
    reshape x1 -> x0, local copies, waits for them, and re-layouts: 41.4 us -> none  [local(): blocks = arrived.reshape(block_count, block_rows, 2, head_count, HD)]
    dot_general x70 -> x0, matrix products: 32.9 us -> none  [the longest x33 13.4 us: block_partial(): jnp.einsum('hsk,khd->shd', weights.astype(jnp.bfloat16), value_rows, pref...]
    while x128 -> x0, local copies, waits for them, and re-layouts: 22 us -> none
  transfers between devices with their start and end apart: 5 -> 0, of which waited for: 5 -> 0; matrix products, arithmetic and copies ran while one was open for 5% -> 0% of each run, Pallas kernels for 0% -> 0%
where the time goes in v1:
time: 109 us
  Pallas kernels  93.5 us (86%)
  local copies, waits for them, and re-layouts  15.2 us (14%)
    pallas_call x1, Pallas kernels, local(): pl.pallas_call(layer_kernel, out_shape=jax.ShapeDtypeStruct((cap, width),...  93.5 us
    slice x1, local copies, waits for them, and re-layouts, local(): gate_up_weight[:, 1]  8.8 us
    squeeze x1, local copies, waits for them, and re-layouts, local(): gate_up_weight[:, 1]  3.17 us

profile of v1, /device:TPU:1, one launch (start us, length us, event | category | flops | bytes accessed | tf_op | source)
XLA Modules:
  0.0 108.7 jit_solution(17033327124686061102)
XLA Ops:
  0.0 8.8 %fusion = (bf16[2048,1,512]{2,1,0:T(2,128)(2,1)S(1)}, bf16[2048,1,512]{2,1,0:T(2,128)(2,1)S(1)}) fusion(bf16[2048,2,512]{2,1,0:T(2,128)(2,1)} %param.15), kind=kLoop, calls=%fused_computation.4 | loop fusion | bytes 8388608 | tf_op jit(solution)/shard_map/slice | solution.py:504
  8.8 0.0 copy-start
  8.8 3.2 %copy_bitcast_fusion = (bf16[2048,512]{1,0:T(8,128)(2,1)}, bf16[2048,512]{1,0:T(8,128)(2,1)}) fusion(bf16[2048,1,512]{2,1,0:T(2,128)(2,1)S(1)} %get-tuple-element.5, bf16[2048,1,512]{2,1,0:T(2,128)(2,1)S(1)} %get-tuple-element.6), kind=kLoop, calls=%fused_computation | loop fusion | bytes 8388608 | tf_op jit(solution)/shard_map/squeeze | solution.py:504
  12.0 0.0 copy-done
  12.0 0.7 fusion.1
  12.7 0.9 copy_bitcast_fusion.2
  13.6 93.5 %layer.1 = bf16[256,256]{1,0:T(8,128)(2,1)} custom-call(bf16[256,256]{1,0:T(8,128)(2,1)} %tok.1, bf16[512,256]{1,0:T(8,128)(2,1)} %get-tuple-element.10.kc, bf16[512,256]{1,0:T(8,128)(2,1)} %get-tuple-element.9.vc, s32[1,128]{1,0:T(1,128)} %bitcast.15, s32[1,128]{1,0:T(1,128)} %bitcast.16, s32[1,128]{1,0:T(1,128)} %bitcast.17, s32[1,128]{1,0:T(1,128)} %bitcast.18, ...), custom_call_target="tpu_custom_call" | custom-call | tf_op jit(solution)/shard_map/layer/pallas_call | solution.py:482
  107.1 1.6 %copy.25 = bf16[256,256]{1,0:T(8,128)(2,1)} copy(bf16[256,256]{1,0:T(8,128)(2,1)} %layer.1) | data formatting | bytes 262144
Async XLA Ops:
  8.8 3.2 %copy-start = (bf16[512,2,256]{2,1,0:T(2,128)(2,1)S(1)}, bf16[512,2,256]{2,1,0:T(2,128)(2,1)}, u32[]{:S(2)}) copy-start(bf16[512,2,256]{2,1,0:T(2,128)(2,1)} %param.12) | copy-start | bytes 1572868

commit v2 on v1

v2 whole, which is shorter than its diff:
```python
import functools
import math

import jax
import jax.numpy as jnp
from jax import lax
from jax.experimental import pallas as pl
from jax.experimental.pallas import tpu as pltpu
from jax.sharding import PartitionSpec as P

HD = 128
NEG = -1e30
EPS = 1e-05
NX, NY, NZ = 4, 4, 8
MESH = pl.DeviceIdType.MESH
F32 = jnp.float32
BF16 = jnp.bfloat16


def dot(a, b):
    return jnp.dot(a, b, preferred_element_type=F32)


def layer_kernel(
    tok, lens, place, group, start, owner, cache, wqkv, wo, wgu, wd,
    out,
    tokg, resg, normed, normed_two, att, hid, cache_v, wqkv_v, wo_v, wgu_v, wd_v, wg_v, wu_v,
    kbuf, vtbuf, qbuf, kloc, vtloc, s_scr, part_acc, part_stat, suf_acc, suf_stat,
    rin_acc, rin_stat, rout_acc, rout_stat, grp_scr, bg_scr,
    pair_out, pair_in, stage, landed, mine, res_own,
    wsem, kv_s, kv_r, q_s, q_r, ra_s, ra_r, rs_s, rs_r,
    ag_s, ag_r, sc_s, sc_r,
):
    cap = tok.shape[0]
    width = tok.shape[1]
    req = lax.axis_index("req")
    mdl = lax.axis_index("mdl")
    z = req // NY
    y = req % NY
    x = mdl // 2
    c = mdl % 2
    xr, xl, xa = (x + 1) % NX, (x + NX - 1) % NX, (x + 2) % NX
    yr, yl, ya = (y + 1) % NY, (y + NY - 1) % NY, (y + 2) % NY
    sib = (req, x * 2 + (1 - c))
    x_right = (req, xr * 2 + c)
    x_left = (req, xl * 2 + c)
    x_far = (req, xa * 2 + c)
    y_right = (z * NY + yr, mdl)
    y_left = (z * NY + yl, mdl)
    z_right = ((z + 1) % NZ * NY + y, mdl)
    z_left = ((z + NZ - 1) % NZ * NY + y, mdl)
    pending = []

    def send(src, dst, s_sem, r_sem, device):
        copy = pltpu.make_async_remote_copy(
            src_ref=src, dst_ref=dst, send_sem=s_sem, recv_sem=r_sem,
            device_id=device, device_id_type=MESH,
        )
        copy.start()
        pending.append(copy)
        return copy

    loads = []
    for i, (src, dst) in enumerate(
        (
            (cache.reshape(cache_v.shape), cache_v),
            (wqkv, wqkv_v),
            (wo, wo_v),
            (wgu.reshape(wgu_v.shape), wgu_v),
            (wd, wd_v),
        )
    ):
        load = pltpu.make_async_copy(src, dst, wsem.at[i])
        load.start()
        loads.append(load)

    barrier = pltpu.get_barrier_semaphore()
    for device in (sib, x_right, x_left, x_far, y_right, y_left, z_right, z_left):
        pl.semaphore_signal(barrier, inc=1, device_id=device, device_id_type=MESH)
    pl.semaphore_wait(barrier, 8)

    class Gather:
        def __init__(self, buf, n):
            self.buf = buf
            self.s, self.r = ag_s.at[n], ag_r.at[n]
            own = buf.at[mdl]
            self.direct = [
                send(own, own, self.s.at[i], self.r.at[i], device)
                for i, device in enumerate((x_far, x_right, x_left, sib))
            ]

        def hand_on(self):
            far, right, left, sibling = self.direct
            self.last = [sibling]
            for i, (copy, origin) in enumerate(((right, xl), (left, xr), (far, xa))):
                copy.wait_recv()
                block = self.buf.at[origin * 2 + c]
                self.last.append(send(block, block, self.s.at[4 + i], self.r.at[4 + i], sib))

        def finish(self):
            for copy in self.last:
                copy.wait_recv()

    class Scatter:
        order = ((xa, x_far), (xr, x_right), (xl, x_left), (x, None))

        def __init__(self, n, chunk):
            self.n, self.chunk = n, chunk
            self.s, self.r = sc_s.at[n], sc_r.at[n]
            self.pairs = []
            for i, (xd, device) in enumerate(self.order):
                pair_out[n, i] = chunk(xd * 2 + (1 - c)).astype(BF16)
                self.pairs.append(
                    send(pair_out.at[n, i], pair_in.at[n, i], self.s.at[i], self.r.at[i], sib)
                )

        def cross(self):
            n = self.n
            self.crossed = []
            for i, (xd, device) in enumerate(self.order):
                own = self.chunk(xd * 2 + c)
                self.pairs[i].wait_recv()
                total = own + pair_in[n, i].astype(F32)
                if device is None:
                    mine[n] = total
                else:
                    stage[n, i] = total.astype(BF16)
                    self.crossed.append(
                        send(
                            stage.at[n, i], landed.at[n, i], self.s.at[4 + i], self.r.at[4 + i],
                            device,
                        )
                    )

        def finish(self):
            total = mine[self.n]
            for i, copy in enumerate(self.crossed):
                copy.wait_recv()
                total = total + landed[self.n, i].astype(F32)
            return total

    def normalize(buf, target):
        rows = buf.shape[1]
        total = jnp.zeros((rows, width), F32)
        for i in range(8):
            total += buf[i].astype(F32)
        mean = jnp.sum(total, axis=1, keepdims=True) * (1.0 / (8 * width))
        square = jnp.zeros((rows, width), F32)
        for i in range(8):
            centered = buf[i].astype(F32) - mean
            square += centered * centered
        var = jnp.sum(square, axis=1, keepdims=True) * (1.0 / (8 * width))
        scale = lax.rsqrt(var + EPS)
        for i in range(8):
            target[:, i * width : (i + 1) * width] = (
                (buf[i].astype(F32) - mean) * scale
            ).astype(BF16)

    tokg[mdl] = tok[...]
    gather_tokens = Gather(tokg, 0)
    taken = lax.broadcasted_iota(jnp.int32, (HD, 2 * HD), 1)
    wanted = lax.broadcasted_iota(jnp.int32, (HD, 2 * HD), 0) * 2
    even = jnp.where(taken == wanted, 1.0, 0.0).astype(BF16)
    odd = jnp.where(taken == wanted + 1, 1.0, 0.0).astype(BF16)
    loads[0].wait()
    block = cache_v.shape[0] // 2
    for h in range(2):
        cols = slice(h * HD, (h + 1) * HD)
        for i in range(block // HD):
            rows = slice(i * 2 * HD, (i + 1) * 2 * HD)
            kbuf[0, h, i * HD : (i + 1) * HD] = dot(even, cache_v[rows, cols]).astype(BF16)
    k_right = send(kbuf.at[0], kbuf.at[1], kv_s.at[0], kv_r.at[0], y_right)
    for h in range(2):
        cols = slice(h * HD, (h + 1) * HD)
        for i in range(block // HD):
            rows = slice(i * 2 * HD, (i + 1) * 2 * HD)
            vtbuf[0, h, :, i * HD : (i + 1) * HD] = jnp.transpose(
                dot(odd, cache_v[rows, cols])
            ).astype(BF16)
    v_left = send(vtbuf.at[0], vtbuf.at[2], kv_s.at[2], kv_r.at[2], y_left)

    count = lens.shape[1]
    ring = lax.broadcasted_iota(jnp.int32, (8, count), 0)
    ring_device = ((z - ring + NZ) % NZ) * NY + y
    placed = place[...] == ring_device
    held = jnp.where(placed, lens[...], 0).astype(F32)
    upper = (
        lax.broadcasted_iota(jnp.int32, (count, count), 0)
        < lax.broadcasted_iota(jnp.int32, (count, count), 1)
    )
    before = dot(held.astype(BF16), jnp.where(upper, 1.0, 0.0).astype(BF16))
    columns = jnp.transpose(
        jnp.concatenate([before, held, jnp.zeros((count - 16, count), F32)], axis=0)
    )
    row = lax.broadcasted_iota(jnp.int32, (8, count), 0)
    request = lax.broadcasted_iota(jnp.int32, (8, count), 1).astype(F32)
    start_high = jnp.right_shift(start[...], 8).astype(F32)
    start_low = jnp.bitwise_and(start[...], 255).astype(F32)
    values = jnp.where(row == 0, 1.0, 0.0)
    values = jnp.where(row == 1, group[...].astype(F32), values)
    values = jnp.where(row == 2, request, values)
    values = jnp.where(row == 3, start_high, values)
    values = jnp.where(row == 4, start_low, values)
    values = jnp.where(row == 5, jnp.broadcast_to(before[0:1], (8, count)), values)
    values = values.astype(BF16)
    slot = lax.broadcasted_iota(jnp.int32, (count, cap), 1).astype(F32)
    for r in range(NZ):
        first = columns[:, r : r + 1]
        size = columns[:, 8 + r : 9 + r]
        belongs = jnp.where((slot >= first) & (slot < first + size), 1.0, 0.0).astype(BF16)
        table = dot(values, belongs)
        slot_group = jnp.where(table[0:1] > 0.5, table[1:2], -1.0)
        grp_scr[r] = jnp.broadcast_to(slot_group, (8, cap))
        if r == 0:
            own_table = table
    occupied = own_table[0:1]
    slot_request = jnp.where(occupied > 0.5, own_table[2:3], -1.0)
    position = (
        own_table[3:4] * 256.0
        + own_table[4:5]
        + (lax.broadcasted_iota(jnp.int32, (1, cap), 1).astype(F32) - own_table[5:6])
    )
    live = jnp.sum(held[0:1], axis=1, keepdims=True)
    blocks = lax.broadcasted_iota(jnp.int32, (1, owner.shape[1]), 1)
    for b, yb in enumerate((y, yl, yr, ya)):
        mine_block = owner[...] == z * NY + yb
        entry = jnp.where(mine_block, jnp.right_shift(blocks, 3), 0).astype(F32)
        bg_scr[b] = jnp.broadcast_to(jnp.sum(entry, axis=1, keepdims=True), (8, cap))
    pair = lax.broadcasted_iota(jnp.int32, (HD // 2, cap), 0).astype(F32)
    frequency = jnp.exp(pair * (-2.0 * math.log(10000.0) / HD))
    angles = position * frequency
    cosine = jnp.cos(angles)
    sine = jnp.sin(angles)

    k_right.wait_send()
    k_left = send(kbuf.at[0], kbuf.at[2], kv_s.at[1], kv_r.at[1], y_left)
    v_left.wait_send()
    v_right = send(vtbuf.at[0], vtbuf.at[1], kv_s.at[3], kv_r.at[3], y_right)
    gather_tokens.hand_on()
    k_right.wait_recv()
    fk = send(kbuf.at[1], kbuf.at[3], kv_s.at[4], kv_r.at[4], y_right)
    v_left.wait_recv()
    fv = send(vtbuf.at[2], vtbuf.at[3], kv_s.at[5], kv_r.at[5], y_left)
    gather_tokens.finish()
    normalize(tokg, normed)
    loads[1].wait()

    def rotated(p, h):
        flat = jnp.transpose(dot(normed[...], wqkv_v[p, :, h * HD : (h + 1) * HD]))
        lower, higher = flat[: HD // 2], flat[HD // 2 :]
        return jnp.concatenate(
            [lower * cosine - higher * sine, higher * cosine + lower * sine], axis=0
        )

    factor = math.log2(math.e) * HD ** (-0.5)
    for h in range(2):
        qbuf[0, h] = (rotated(0, h) * factor).astype(BF16)

    q_copies = {}

    def q_send(d, k, h):
        if d == 0:
            source, target, device = qbuf.at[k - 1, h], qbuf.at[k, h], z_right
        else:
            source, target, device = qbuf.at[(NZ + 1 - k) % NZ, h], qbuf.at[NZ - k, h], z_left
        q_copies[d, k, h] = send(source, target, q_s.at[d, k, h], q_r.at[d, k, h], device)

    lanes = ((0, 0), (1, 1), (0, 1), (1, 0))

    def q_pass(k):
        for d, h in lanes:
            if (d, k, h) in q_copies:
                q_copies[d, k, h].wait_recv()
                if k < 3 or (k == 3 and d == h):
                    q_send(d, k + 1, h)

    for d, h in lanes:
        q_send(d, 1, h)

    for h in range(2):
        kloc[h] = jnp.transpose(rotated(1, h)).astype(BF16)
        vtloc[h] = jnp.transpose(dot(normed[...], wqkv_v[2, :, h * HD : (h + 1) * HD])).astype(BF16)

    def put_stat(ref, top, weight):
        which = lax.broadcasted_iota(jnp.int32, (8, cap), 0)
        ref[...] = jnp.where(which == 0, top, jnp.where(which == 1, weight, 0.0))

    request_column = jnp.transpose(jnp.broadcast_to(slot_request, (HD, cap)))[:, 0:1]
    key_slot = lax.broadcasted_iota(jnp.int32, (cap, cap), 0)
    query_slot = lax.broadcasted_iota(jnp.int32, (cap, cap), 1)
    causal = (request_column == slot_request) & (key_slot <= query_slot) & (slot_request >= 0.0)
    for h in range(2):
        scores = jnp.where(causal, dot(kloc[h], qbuf[0, h]), NEG)
        top = jnp.max(scores, axis=0, keepdims=True)
        weights = jnp.where(causal, jnp.exp2(scores - top), 0.0)
        suf_acc[h] = dot(vtloc[h], weights.astype(BF16))
        put_stat(suf_stat.at[h], top, jnp.sum(weights, axis=0, keepdims=True))

    def near_blocks(r, h):
        query = qbuf[r, h]
        slot_groups = grp_scr[r]
        top = jnp.full((8, cap), NEG, F32)
        for b in range(3):
            scores = dot(kbuf[b, h], query)
            s_scr[b] = scores
            best = jnp.broadcast_to(jnp.max(scores, axis=0, keepdims=True), (8, cap))
            top = jnp.maximum(top, jnp.where(slot_groups == bg_scr[b], best, NEG))
        total = jnp.zeros((1, cap), F32)
        acc = jnp.zeros((HD, cap), F32)
        for b in range(3):
            shift = jnp.where(slot_groups == bg_scr[b], top, -NEG)[0:1]
            weights = jnp.exp2(s_scr[b] - shift)
            total += jnp.sum(weights, axis=0, keepdims=True)
            acc += dot(vtbuf[b, h], weights.astype(BF16))
        part_acc[r, h] = acc
        put_stat(part_stat.at[r, h], top[0:1], total)

    def far_block(r, h):
        same = grp_scr[r] == bg_scr[3]
        scores = dot(kbuf[3, h], qbuf[r, h])
        best = jnp.broadcast_to(jnp.max(scores, axis=0, keepdims=True), (8, cap))
        old = part_stat[r, h, 0:1]
        top = jnp.maximum(old, jnp.where(same, best, NEG)[0:1])
        weights = jnp.exp2(scores - jnp.where(same[0:1], top, -NEG))
        scale = jnp.exp2(old - top)
        total = part_stat[r, h, 1:2] * scale + jnp.sum(weights, axis=0, keepdims=True)
        acc = part_acc[r, h] * scale + dot(vtbuf[3, h], weights.astype(BF16))
        part_acc[r, h] = acc
        put_stat(part_stat.at[r, h], top, total)

    def for_both(k, step):
        def body(i, carry):
            step(jnp.where(i < 2, k, NZ - k), i % 2)
            return carry

        lax.fori_loop(0, 4, body, 0)

    def for_heads(r, step):
        def body(h, carry):
            step(r, h)
            return carry

        lax.fori_loop(0, 2, body, 0)

    q_pass(1)
    k_left.wait_recv()
    v_right.wait_recv()
    for_heads(0, near_blocks)
    q_pass(2)
    for_both(1, near_blocks)
    q_pass(3)
    for_both(2, near_blocks)
    q_pass(4)
    for_heads(4, near_blocks)
    fk.wait_recv()
    fv.wait_recv()

    def combine(parts):
        top = parts[0][1]
        for part in parts[1:]:
            top = jnp.maximum(top, part[1])
        acc, total = 0.0, 0.0
        for part in parts:
            scale = jnp.exp2(part[1] - top)
            acc = acc + part[0] * scale
            total = total + part[2] * scale
        return acc, top, total

    back = {}

    def own_part(r, h):
        return part_acc[r, h], part_stat[r, h, 0:1], part_stat[r, h, 1:2]

    def arrived(d, k, h):
        for copy in back[d, k, h]:
            copy.wait_recv()
        return rin_acc[d, k, h].astype(F32), rin_stat[d, k, h, 0:1], rin_stat[d, k, h, 1:2]

    def back_step(d, k, h):
        parts = [own_part(NZ - k if d == 0 else k, h)]
        if (d, k + 1, h) in back:
            parts.append(arrived(d, k + 1, h))
        acc, top, total = combine(parts)
        rout_acc[d, k, h] = acc.astype(BF16)
        put_stat(rout_stat.at[d, k, h], top, total)
        device = z_right if d == 0 else z_left
        back[d, k, h] = (
            send(rout_acc.at[d, k, h], rin_acc.at[d, k, h], ra_s.at[d, k, h], ra_r.at[d, k, h], device),
            send(rout_stat.at[d, k, h], rin_stat.at[d, k, h], rs_s.at[d, k, h], rs_r.at[d, k, h], device),
        )

    far_block(4, 0)
    back_step(0, 4, 0)
    far_block(4, 1)
    back_step(1, 4, 1)
    for_both(3, near_blocks)
    for_both(3, far_block)
    for d, h in ((0, 1), (1, 0), (0, 0), (1, 1)):
        back_step(d, 3, h)
    for_both(2, far_block)
    for d, h in lanes:
        back_step(d, 2, h)
    for_both(1, far_block)
    for d, h in lanes:
        back_step(d, 1, h)
    for_heads(0, far_block)
    rows = []
    for h in range(2):
        parts = [
            (suf_acc[h], suf_stat[h, 0:1], suf_stat[h, 1:2]),
            (part_acc[0, h], part_stat[0, h, 0:1], part_stat[0, h, 1:2]),
        ]
        parts += [arrived(0, 1, h), arrived(1, 1, h)]
        acc, top, total = combine(parts)
        some = total > 0.0
        rows.append(jnp.where(some, acc / jnp.where(some, total, 1.0), 0.0))
    attention = jnp.transpose(jnp.concatenate(rows, axis=0)).astype(BF16)

    half = cap // 2
    halves = (0, 1)
    for i in halves:
        att[i] = attention[i * half : (i + 1) * half]
    loads[2].wait()

    def columns_of(weight, m):
        return weight[:, pl.ds(pl.multiple_of(m * width, width), width)]

    scatters = [Scatter(i, lambda m, i=i: dot(att[i], columns_of(wo_v, m))) for i in halves]
    for scatter in scatters:
        scatter.cross()
    loads[3].wait()
    loads[4].wait()

    def split(i, carry):
        pairs = wgu_v[pl.ds(i * 2 * HD, 2 * HD)]
        wg_v[pl.ds(i * HD, HD)] = dot(even, pairs).astype(BF16)
        wu_v[pl.ds(i * HD, HD)] = dot(odd, pairs).astype(BF16)
        return carry

    lax.fori_loop(0, wg_v.shape[0] // HD, split, 0)
    gathers = []
    for i in halves:
        own = tok[i * half : (i + 1) * half].astype(F32) + scatters[i].finish()
        resg[i, mdl] = own.astype(BF16)
        res_own[i] = own.astype(BF16)
        gathers.append(Gather(resg.at[i], 1 + i))
    for gather in gathers:
        gather.hand_on()
    scatters = []
    for i in halves:
        gathers[i].finish()
        normalize(resg.at[i], normed_two.at[i])
        gate = dot(normed_two[i], wg_v[...])
        up = dot(normed_two[i], wu_v[...])
        hid[i] = (gate / (1.0 + jnp.exp(-gate)) * up).astype(BF16)
        scatters.append(Scatter(2 + i, lambda m, i=i: dot(hid[i], columns_of(wd_v, m))))
    for scatter in scatters:
        scatter.cross()
    index = lax.broadcasted_iota(jnp.int32, (half, width), 0).astype(F32)
    for i in halves:
        finished = res_own[i].astype(F32) + scatters[i].finish()
        out[i * half : (i + 1) * half] = jnp.where(
            index + float(i * half) < live, finished, 0.0
        ).astype(BF16)
    for copy in pending:
        if copy is not k_right and copy is not v_left:
            copy.wait_send()


def local(
    tokens, prefix_cache, qkv_weight, out_weight, gate_up_weight, down_weight,
    lengths, placement, request_group, block_owner, start_position,
):
    cap, width = tokens.shape
    block = prefix_cache.shape[0]
    model = qkv_weight.shape[0]
    hidden = down_weight.shape[0]
    vmem = pl.BlockSpec(memory_space=pltpu.VMEM)
    hbm = pl.BlockSpec(memory_space=pl.ANY)
    dma = pltpu.SemaphoreType.DMA
    half = cap // 2
    ring = (2, 5, 2)
    scratch = [
        pltpu.VMEM((8, cap, width), BF16),
        pltpu.VMEM((2, 8, half, width), BF16),
        pltpu.VMEM((cap, model), BF16),
        pltpu.VMEM((2, half, model), BF16),
        pltpu.VMEM((2, half, width), BF16),
        pltpu.VMEM((2, half, hidden), BF16),
        pltpu.VMEM((2 * block, width), BF16),
        pltpu.VMEM((3, model, width), BF16),
        pltpu.VMEM((width, model), BF16),
        pltpu.VMEM((2 * model, hidden), BF16),
        pltpu.VMEM((hidden, model), BF16),
        pltpu.VMEM((model, hidden), BF16),
        pltpu.VMEM((model, hidden), BF16),
        pltpu.VMEM((NY, 2, block, HD), BF16),
        pltpu.VMEM((NY, 2, HD, block), BF16),
        pltpu.VMEM((NZ, 2, HD, cap), BF16),
        pltpu.VMEM((2, cap, HD), BF16),
        pltpu.VMEM((2, HD, cap), BF16),
        pltpu.VMEM((3, block, cap), F32),
        pltpu.VMEM((NZ, 2, HD, cap), F32),
        pltpu.VMEM((NZ, 2, 8, cap), F32),
        pltpu.VMEM((2, HD, cap), F32),
        pltpu.VMEM((2, 8, cap), F32),
        pltpu.VMEM(ring + (HD, cap), BF16),
        pltpu.VMEM(ring + (8, cap), F32),
        pltpu.VMEM(ring + (HD, cap), BF16),
        pltpu.VMEM(ring + (8, cap), F32),
        pltpu.VMEM((NZ, 8, cap), F32),
        pltpu.VMEM((NY, 8, cap), F32),
        pltpu.VMEM((4, 4, half, width), BF16),
        pltpu.VMEM((4, 4, half, width), BF16),
        pltpu.VMEM((4, 3, half, width), BF16),
        pltpu.VMEM((4, 3, half, width), BF16),
        pltpu.VMEM((4, half, width), F32),
        pltpu.VMEM((2, half, width), BF16),
        dma((5,)),
        dma((6,)), dma((6,)),
        dma(ring), dma(ring),
        dma(ring), dma(ring), dma(ring), dma(ring),
        dma((3, 7)), dma((3, 7)), dma((4, 7)), dma((4, 7)),
    ]
    return pl.pallas_call(
        layer_kernel,
        out_shape=jax.ShapeDtypeStruct((cap, width), BF16),
        in_specs=[vmem] * 6 + [hbm] * 5,
        out_specs=vmem,
        scratch_shapes=scratch,
        compiler_params=pltpu.CompilerParams(
            collective_id=0, has_side_effects=True, vmem_limit_bytes=58 << 20
        ),
        name="layer",
    )(
        tokens,
        lengths.reshape(1, -1),
        placement.reshape(1, -1),
        request_group.reshape(1, -1),
        start_position.reshape(1, -1),
        block_owner.reshape(1, -1),
        prefix_cache,
        jnp.transpose(qkv_weight, (1, 0, 2)),
        out_weight,
        gate_up_weight,
        down_weight,
    )


def solution(mesh):
    in_specs = (
        P("req", "mdl"),
        P("req", None, "mdl"),
        P(None, None, "mdl"),
        P("mdl", None),
        P(None, None, "mdl"),
        P("mdl", None),
        P(),
        P(),
        P(),
        P(),
        P(),
    )
    return jax.shard_map(
        local, mesh=mesh, in_specs=in_specs, out_specs=P("req", "mdl"), check_vma=False
    )
```

time: 109 us -> 90.3 us (0.83)
  local copies, waits for them, and re-layouts: 15.2 us -> 1.57 us
  Pallas kernels: 93.5 us -> 88.6 us
    slice x2 -> x0, local copies, waits for them, and re-layouts: 9.53 us -> none  [the longest x1 8.8 us: local(): gate_up_weight[:, 1]]
    pallas_call x1, Pallas kernels: 93.5 us -> 88.6 us  [local(): pl.pallas_call(layer_kernel, out_shape=jax.ShapeDtypeStruct((cap, width),...]
    squeeze x2 -> x0, local copies, waits for them, and re-layouts: 4.09 us -> none  [the longest x1 3.17 us: local(): gate_up_weight[:, 1]]
where the time goes in v2:
time: 90.3 us; the launch traced here: 90.2 us
  Pallas kernels  88.6 us (98%)
  local copies, waits for them, and re-layouts  1.57 us (2%)
    pallas_call x1, Pallas kernels, local(): pl.pallas_call(layer_kernel, out_shape=jax.ShapeDtypeStruct((cap, width),...  88.6 us

profile of v2, /device:TPU:1, one launch (start us, length us, event | category | flops | bytes accessed | tf_op | source)
XLA Modules:
  0.0 90.2 jit_solution(1436308809199524825)
XLA Ops:
  0.0 88.6 %layer.1 = bf16[256,256]{1,0:T(8,128)(2,1)} custom-call(bf16[256,256]{1,0:T(8,128)(2,1)} %tok.1, s32[1,128]{1,0:T(1,128)} %bitcast.7, s32[1,128]{1,0:T(1,128)} %bitcast.8, s32[1,128]{1,0:T(1,128)} %bitcast.9, s32[1,128]{1,0:T(1,128)} %bitcast.10, s32[1,32]{1,0:T(1,128)} %bitcast.11, bf16[512,2,256]{2,1,0:T(2,128)(2,1)} %cache.1, ...), custom_call_target="tpu_custom_call" | custom-call | tf_op jit(solution)/shard_map/layer/pallas_call | solution.py:525
  88.6 1.6 %copy.13 = bf16[256,256]{1,0:T(8,128)(2,1)} copy(bf16[256,256]{1,0:T(8,128)(2,1)} %layer.1) | data formatting | bytes 262144

commit v3 on v2

--- a/solution.py
+++ b/solution.py
@@ -86,11 +86,11 @@
             own = buf.at[mdl]
             self.direct = [
                 send(own, own, self.s.at[i], self.r.at[i], device)
-                for i, device in enumerate((x_far, x_right, x_left, sib))
+                for i, device in enumerate((x_right, x_left, sib, x_far))
             ]
 
         def hand_on(self):
-            far, right, left, sibling = self.direct
+            right, left, sibling, far = self.direct
             self.last = [sibling]
             for i, (copy, origin) in enumerate(((right, xl), (left, xr), (far, xa))):
                 copy.wait_recv()
@@ -102,7 +102,7 @@
                 copy.wait_recv()
 
     class Scatter:
-        order = ((xa, x_far), (xr, x_right), (xl, x_left), (x, None))
+        order = ((xr, x_right), (xl, x_left), (xa, x_far), (x, None))
 
         def __init__(self, n, chunk):
             self.n, self.chunk = n, chunk
@@ -277,24 +277,9 @@
     for d, h in lanes:
         q_send(d, 1, h)
 
-    for h in range(2):
-        kloc[h] = jnp.transpose(rotated(1, h)).astype(BF16)
-        vtloc[h] = jnp.transpose(dot(normed[...], wqkv_v[2, :, h * HD : (h + 1) * HD])).astype(BF16)
-
     def put_stat(ref, top, weight):
         which = lax.broadcasted_iota(jnp.int32, (8, cap), 0)
         ref[...] = jnp.where(which == 0, top, jnp.where(which == 1, weight, 0.0))
-
-    request_column = jnp.transpose(jnp.broadcast_to(slot_request, (HD, cap)))[:, 0:1]
-    key_slot = lax.broadcasted_iota(jnp.int32, (cap, cap), 0)
-    query_slot = lax.broadcasted_iota(jnp.int32, (cap, cap), 1)
-    causal = (request_column == slot_request) & (key_slot <= query_slot) & (slot_request >= 0.0)
-    for h in range(2):
-        scores = jnp.where(causal, dot(kloc[h], qbuf[0, h]), NEG)
-        top = jnp.max(scores, axis=0, keepdims=True)
-        weights = jnp.where(causal, jnp.exp2(scores - top), 0.0)
-        suf_acc[h] = dot(vtloc[h], weights.astype(BF16))
-        put_stat(suf_stat.at[h], top, jnp.sum(weights, axis=0, keepdims=True))
 
     def near_blocks(r, h):
         query = qbuf[r, h]
@@ -404,6 +389,22 @@
     for d, h in lanes:
         back_step(d, 1, h)
     for_heads(0, far_block)
+
+    for h in range(2):
+        kloc[h] = jnp.transpose(rotated(1, h)).astype(BF16)
+        vtloc[h] = jnp.transpose(dot(normed[...], wqkv_v[2, :, h * HD : (h + 1) * HD])).astype(BF16)
+
+    request_column = jnp.transpose(jnp.broadcast_to(slot_request, (HD, cap)))[:, 0:1]
+    key_slot = lax.broadcasted_iota(jnp.int32, (cap, cap), 0)
+    query_slot = lax.broadcasted_iota(jnp.int32, (cap, cap), 1)
+    causal = (request_column == slot_request) & (key_slot <= query_slot) & (slot_request >= 0.0)
+    for h in range(2):
+        scores = jnp.where(causal, dot(kloc[h], qbuf[0, h]), NEG)
+        top = jnp.max(scores, axis=0, keepdims=True)
+        weights = jnp.where(causal, jnp.exp2(scores - top), 0.0)
+        suf_acc[h] = dot(vtloc[h], weights.astype(BF16))
+        put_stat(suf_stat.at[h], top, jnp.sum(weights, axis=0, keepdims=True))
+
     rows = []
     for h in range(2):
         parts = [

time: 90.3 us -> 89.6 us (level)
  no operation moved by 1% of the time
where the time goes in v3:
time: 89.6 us; the launch traced here: 89.5 us
  Pallas kernels  87.9 us (98%)
  local copies, waits for them, and re-layouts  1.57 us (2%)
    pallas_call x1, Pallas kernels, local(): pl.pallas_call(layer_kernel, out_shape=jax.ShapeDtypeStruct((cap, width),...  87.9 us

profile of v3, /device:TPU:1, one launch (start us, length us, event | category | flops | bytes accessed | tf_op | source)
XLA Modules:
  0.0 89.5 jit_solution(15476383949269830979)
XLA Ops:
  0.0 87.9 %layer.1 = bf16[256,256]{1,0:T(8,128)(2,1)} custom-call(bf16[256,256]{1,0:T(8,128)(2,1)} %tok.1, s32[1,128]{1,0:T(1,128)} %bitcast.7, s32[1,128]{1,0:T(1,128)} %bitcast.8, s32[1,128]{1,0:T(1,128)} %bitcast.9, s32[1,128]{1,0:T(1,128)} %bitcast.10, s32[1,32]{1,0:T(1,128)} %bitcast.11, bf16[512,2,256]{2,1,0:T(2,128)(2,1)} %cache.1, ...), custom_call_target="tpu_custom_call" | custom-call | tf_op jit(solution)/shard_map/layer/pallas_call | solution.py:526
  88.0 1.6 %copy.13 = bf16[256,256]{1,0:T(8,128)(2,1)} copy(bf16[256,256]{1,0:T(8,128)(2,1)} %layer.1) | data formatting | bytes 262144

commit v4 on v3

--- a/solution.py
+++ b/solution.py
@@ -320,6 +320,13 @@
 
         lax.fori_loop(0, 4, body, 0)
 
+    def for_one(k, h, step):
+        def body(i, carry):
+            step(jnp.where(i == 0, k, NZ - k), h)
+            return carry
+
+        lax.fori_loop(0, 2, body, 0)
+
     def for_heads(r, step):
         def body(h, carry):
             step(r, h)
@@ -334,7 +341,7 @@
     q_pass(2)
     for_both(1, near_blocks)
     q_pass(3)
-    for_both(2, near_blocks)
+    for_both(3, near_blocks)
     q_pass(4)
     for_heads(4, near_blocks)
     fk.wait_recv()
@@ -378,10 +385,13 @@
     back_step(0, 4, 0)
     far_block(4, 1)
     back_step(1, 4, 1)
-    for_both(3, near_blocks)
     for_both(3, far_block)
-    for d, h in ((0, 1), (1, 0), (0, 0), (1, 1)):
-        back_step(d, 3, h)
+    back_step(0, 3, 1)
+    back_step(1, 3, 0)
+    for_one(2, 0, near_blocks)
+    back_step(0, 3, 0)
+    back_step(1, 3, 1)
+    for_one(2, 1, near_blocks)
     for_both(2, far_block)
     for d, h in lanes:
         back_step(d, 2, h)

time: 89.6 us -> 87.9 us (0.981)
  Pallas kernels: 87.9 us -> 86.2 us
    pallas_call x1, Pallas kernels: 87.9 us -> 86.2 us  [local(): pl.pallas_call(layer_kernel, out_shape=jax.ShapeDtypeStruct((cap, width),...]
where the time goes in v4:
time: 87.9 us; the launch traced here: 87.8 us
  Pallas kernels  86.2 us (98%)
  local copies, waits for them, and re-layouts  1.57 us (2%)
    pallas_call x1, Pallas kernels, local(): pl.pallas_call(layer_kernel, out_shape=jax.ShapeDtypeStruct((cap, width),...  86.2 us

profile of v4, /device:TPU:1, one launch (start us, length us, event | category | flops | bytes accessed | tf_op | source)
XLA Modules:
  0.0 87.8 jit_solution(3275742090506225127)
XLA Ops:
  0.0 86.2 %layer.1 = bf16[256,256]{1,0:T(8,128)(2,1)} custom-call(bf16[256,256]{1,0:T(8,128)(2,1)} %tok.1, s32[1,128]{1,0:T(1,128)} %bitcast.7, s32[1,128]{1,0:T(1,128)} %bitcast.8, s32[1,128]{1,0:T(1,128)} %bitcast.9, s32[1,128]{1,0:T(1,128)} %bitcast.10, s32[1,32]{1,0:T(1,128)} %bitcast.11, bf16[512,2,256]{2,1,0:T(2,128)(2,1)} %cache.1, ...), custom_call_target="tpu_custom_call" | custom-call | tf_op jit(solution)/shard_map/layer/pallas_call | solution.py:536
  86.2 1.6 %copy.13 = bf16[256,256]{1,0:T(8,128)(2,1)} copy(bf16[256,256]{1,0:T(8,128)(2,1)} %layer.1) | data formatting | bytes 262144
